TPU v7x, 32 devices: a whole 2x2x4 slice. The times are simulated.
32 devices in a mesh: groups: 2 (over y), ctx: 4 (over z), mp: 4 (over x, core).
Axes of the slice: x: 2, y: 2, z: 4, core: 2. Of those that a mesh axis runs over, the one named last changes fastest.
Arguments:
- queries: bfloat16 [2048, 4096], P(('groups', 'ctx'), 'mp'), parts along dimension 0, may hold values from -18 to 18
- keyvals: bfloat16 [2048, 512], P(('groups', 'ctx', 'mp')), parts along dimension 0, may hold values from -6 to 6
- segment_ids: int32 [2048], P('groups'), parts along dimension 0, may hold values from 0 to 2, never falling along the last dimension, each value on 1 to 512 neighbouring positions
- residual: bfloat16 [2048, 4096], P(('groups', 'ctx', 'mp')), parts along dimension 0, may hold values from -180 to 180
- out_weight: bfloat16 [4096, 4096], P('mp', 'ctx'), may hold values from -0.375 to 0.375
- lru_weight: bfloat16 [4096, 4096], P('ctx', 'mp'), may hold values from -0.09375 to 0.09375
- conv_weight: float32 [4, 4096], P(None, 'mp'), may hold values from -3 to 3
- gate_decay_w: bfloat16 [16, 256, 256], P('mp'), may hold values from -0.375 to 0.375
- gate_input_w: bfloat16 [16, 256, 256], P('mp'), may hold values from -0.375 to 0.375
- gate_decay_b: float32 [4096], P('mp'), may hold values from -3 to 3
- gate_input_b: float32 [4096], P('mp'), may hold values from -3 to 3
- decay_codes: int32 [4096], P('mp'), may hold values from 0 to 15
- norm_gain: float32 [4096], replicated, may hold values from 0.1 to 1.9
Outputs:
- resid_out: bfloat16 [2048, 4096], P(('groups', 'ctx', 'mp')), parts along dimension 0
- lru_out: bfloat16 [2048, 4096], P(('groups', 'ctx'), 'mp'), parts along dimension 0
There are 2 independent parts, one for each index of `groups`. A program takes and returns all parts, laid end to end along the dimension named above; an argument that names none is the same for every part. Nothing has to cross between parts.
All inputs are finite; a program needn't handle non-finite values.
Results may differ from a plain program's by a relative error of at most 0.017.
Values may be sent and summed in bfloat16 or wider, within the bound.
No kernel may reach another device: no remote copies, remote signals or barrier semaphores. Data moves between devices by JAX's collectives and lax.ppermute only.
A program may use at most 64 MiB of HBM per device.

v0:
```python
import math
import jax
import jax.numpy as jnp
from jax import lax
from jax.sharding import PartitionSpec as P

HD = 256
WIN = 2048
CONV = 4
LEVELS = 16
BW = 256


def shifted_2(value, axis, steps):
    count = lax.axis_size(axis)
    initial, last = (max(0, -steps), min(count, count - steps))
    return lax.ppermute(value, axis, [(source, source + steps) for source in range(initial, last)])


def decay_rates():
    levels = jnp.arange(LEVELS, dtype=jnp.float32)
    return 0.006 * jnp.exp(-levels * (math.log(3000.0) / (LEVELS - 1)))


def chain_link(former, latter):
    return (former[0] * latter[0], latter[0] * former[1] + latter[1])


def rms_scaled(values, norm_gain):
    value_f32 = values.astype(jnp.float32)
    inverse = lax.rsqrt(jnp.mean(value_f32 * value_f32, axis=-1, keepdims=True) + 1e-06)
    return (value_f32 * inverse * norm_gain).astype(jnp.bfloat16)


def attend_local(queries, keys_all, allowed):
    rows_here = queries.shape[0]
    heads_here = queries.shape[1] // HD
    query_heads = queries.reshape(rows_here, heads_here, HD)
    score_scale = 1.0 / math.sqrt(HD)
    scores = (
        jnp.einsum("thd,kd->htk", query_heads, keys_all[:, :HD], preferred_element_type=jnp.float32)
        * score_scale
    )
    scores = jnp.where(allowed[None], scores, -1e30)
    row_top = jnp.max(scores, axis=-1, keepdims=True)
    weights = jnp.exp(scores - row_top)
    probs = (weights / jnp.sum(weights, axis=-1, keepdims=True)).astype(jnp.bfloat16)
    gathered = jnp.einsum(
        "htk,kd->thd", probs, keys_all[:, HD:], preferred_element_type=jnp.float32
    )
    return gathered.reshape(rows_here, heads_here * HD).astype(jnp.bfloat16)


def local(
    queries,
    keyvals,
    segment_ids,
    residual,
    out_weight,
    lru_weight,
    conv_weight,
    gate_decay_w,
    gate_input_w,
    gate_decay_b,
    gate_input_b,
    decay_codes,
    norm_gain,
):
    rows_here = queries.shape[0]
    ctx_index = lax.axis_index("ctx")
    back_blocks = WIN // rows_here
    own_kv = lax.all_gather(keyvals, "mp", axis=0, tiled=True)
    earlier = []
    moving = own_kv
    for offset in range(back_blocks):
        moving = shifted_2(moving, "ctx", 1)
        earlier = [moving] + earlier
    keys_all = jnp.concatenate(earlier + [own_kv], axis=0)
    pad_seg = jnp.concatenate([jnp.full((WIN,), -1, jnp.int32), segment_ids])
    query_seg = lax.dynamic_slice_in_dim(segment_ids, ctx_index * rows_here, rows_here)
    key_seg = lax.dynamic_slice_in_dim(
        pad_seg, ctx_index * rows_here, (back_blocks + 1) * rows_here
    )
    query_pos = ctx_index * rows_here + jnp.arange(rows_here, dtype=jnp.int32)
    key_pos = (ctx_index - back_blocks) * rows_here + jnp.arange(
        (back_blocks + 1) * rows_here, dtype=jnp.int32
    )
    distance = query_pos[:, None] - key_pos[None, :]
    allowed = (distance >= 0) & (distance < WIN) & (query_seg[:, None] == key_seg[None, :])
    attended = attend_local(queries, keys_all, allowed)
    head_part = jnp.dot(
        attended,
        lax.all_gather(out_weight, "ctx", axis=1, tiled=True),
        preferred_element_type=jnp.float32,
    )
    summed = lax.psum_scatter(
        head_part.astype(jnp.bfloat16), "mp", scatter_dimension=0, tiled=True
    ).astype(jnp.float32)
    resid_out = (summed + residual.astype(jnp.float32)).astype(jnp.bfloat16)
    normed = lax.all_gather(rms_scaled(resid_out, norm_gain), "mp", axis=0, tiled=True)
    channels = lru_weight.shape[1]
    lru_in = jnp.dot(
        normed,
        lax.all_gather(lru_weight, "ctx", axis=0, tiled=True),
        preferred_element_type=jnp.float32,
    ).astype(jnp.bfloat16)
    rim_rows = shifted_2(lru_in[rows_here - (CONV - 1) :], "ctx", 1)
    extended = jnp.concatenate([rim_rows, lru_in], axis=0)
    ext_seg = lax.dynamic_slice_in_dim(
        pad_seg, ctx_index * rows_here + WIN - (CONV - 1), rows_here + CONV - 1
    )
    conv_acc = jnp.zeros((rows_here, channels), jnp.float32)
    for offset in range(CONV):
        lag_rows = CONV - 1 - offset
        shifted = extended[lag_rows : lag_rows + rows_here].astype(jnp.float32)
        same_doc = (ext_seg[lag_rows : lag_rows + rows_here] == query_seg)[:, None]
        conv_acc = conv_acc + jnp.where(same_doc, conv_weight[offset] * shifted, 0.0)
    conv_out = conv_acc.astype(jnp.bfloat16)
    blocks_here = channels // BW
    grouped = conv_out.reshape(rows_here, blocks_here, BW)
    decay_gate = jax.nn.sigmoid(
        jnp.einsum(
            "tbi,bij->tbj", grouped, gate_decay_w, preferred_element_type=jnp.float32
        ).reshape(rows_here, channels)
        + gate_decay_b
    )
    input_gate = jax.nn.sigmoid(
        jnp.einsum(
            "tbi,bij->tbj", grouped, gate_input_w, preferred_element_type=jnp.float32
        ).reshape(rows_here, channels)
        + gate_input_b
    )
    levels = jnp.arange(LEVELS, dtype=jnp.int32)
    decay_rate = jnp.sum(
        jnp.where(decay_codes[:, None] == levels[None, :], decay_rates()[None, :], 0.0), axis=1
    )
    log_decay = -8.0 * decay_gate * decay_rate
    restart = (query_seg != ext_seg[CONV - 2 : CONV - 2 + rows_here])[:, None]
    keep_factor = jnp.where(restart, 0.0, jnp.exp(log_decay))
    input_scale = jnp.where(restart, 1.0, jnp.sqrt(-jnp.expm1(2.0 * log_decay)))
    driven = input_scale * input_gate * conv_out.astype(jnp.float32)
    cum_keep, local_state = lax.associative_scan(chain_link, (keep_factor, driven), axis=0)
    block_keep = cum_keep[rows_here - 1]
    block_state = local_state[rows_here - 1]

    def relay_turn(turn_index, state_in):
        return shifted_2(block_keep * state_in + block_state, "ctx", 1)

    incoming = lax.fori_loop(0, lax.axis_size("ctx") - 1, relay_turn, jnp.zeros_like(block_state))
    states = local_state + cum_keep * incoming[None, :]
    return (resid_out, states.astype(jnp.bfloat16))


def solution(mesh):
    in_specs = (
        P(("groups", "ctx"), "mp"),
        P(("groups", "ctx", "mp"), None),
        P("groups"),
        P(("groups", "ctx", "mp"), None),
        P("mp", "ctx"),
        P("ctx", "mp"),
        P(None, "mp"),
        P("mp", None, None),
        P("mp", None, None),
        P("mp"),
        P("mp"),
        P("mp"),
        P(),
    )
    out_specs = (P(("groups", "ctx", "mp"), None), P(("groups", "ctx"), "mp"))
    return jax.shard_map(local, mesh=mesh, in_specs=in_specs, out_specs=out_specs, check_vma=False)
```

profile of v0, /device:TPU:0, one launch (start us, length us, event | category | flops | bytes accessed | tf_op | source)
XLA Modules:
  0.0 554.3 jit_solution(5232723126797398906)
XLA Ops:
  8.0 7.4 %all_gather.12 = bf16[256,512]{1,0:T(8,128)(2,1)S(1)} all-gather(bf16[64,512]{1,0:T(8,128)(2,1)} %param.16), channel_id=1, replica_groups=mesh['groups'=2,'ctx'=4,'mp'=4] {'mp'}, dimensions={0}, use_global_device_ids=true | all-gather | bytes 327680 | tf_op jit(solution)/shard_map/all_gather | solution.py:72
  18.9 9.3 %collective-permute-done.1 = bf16[256,512]{1,0:T(8,128)(2,1)S(1)} collective-permute-done((bf16[256,512]{1,0:T(8,128)(2,1)S(1)}, bf16[256,512]{1,0:T(8,128)(2,1)S(1)}, u32[]{:S(2)}, u32[]{:S(2)}) %collective-permute-start.1) | collective-permute-done | bytes 262176 | tf_op jit(solution)/shard_map/ppermute | solution.py:17
  28.3 8.5 %collective-permute-start.2 = (bf16[256,512]{1,0:T(8,128)(2,1)S(1)}, bf16[256,512]{1,0:T(8,128)(2,1)S(1)}, u32[]{:S(2)}, u32[]{:S(2)}) collective-permute-start(bf16[256,512]{1,0:T(8,128)(2,1)S(1)} %collective-permute-done.1), channel_id=1, source_target_pairs={{0,4},{4,8},{8,12},{1,5},{5,9},{9,13},{2,6},{6,10},{10,14},{3,7},{... | collective-permute-start | bytes 786440 | tf_op jit(solution)/shard_map/ppermute | solution.py:17
  36.8 11.2 %collective-permute-done.2 = bf16[256,512]{1,0:T(8,128)(2,1)S(1)} collective-permute-done((bf16[256,512]{1,0:T(8,128)(2,1)S(1)}, bf16[256,512]{1,0:T(8,128)(2,1)S(1)}, u32[]{:S(2)}, u32[]{:S(2)}) %collective-permute-start.2) | collective-permute-done | bytes 262176 | tf_op jit(solution)/shard_map/ppermute | solution.py:17
  48.0 13.6 %collective-permute-start.3 = (bf16[256,512]{1,0:T(8,128)(2,1)S(1)}, bf16[256,512]{1,0:T(8,128)(2,1)S(1)}, u32[]{:S(2)}, u32[]{:S(2)}) collective-permute-start(bf16[256,512]{1,0:T(8,128)(2,1)S(1)} %collective-permute-done.2), channel_id=1, source_target_pairs={{0,4},{4,8},{8,12},{1,5},{5,9},{9,13},{2,6},{6,10},{10,14},{3,7},{... | collective-permute-start | bytes 786440 | tf_op jit(solution)/shard_map/ppermute | solution.py:17
  61.6 10.2 %collective-permute-done.3 = bf16[256,512]{1,0:T(8,128)(2,1)S(1)} collective-permute-done((bf16[256,512]{1,0:T(8,128)(2,1)S(1)}, bf16[256,512]{1,0:T(8,128)(2,1)S(1)}, u32[]{:S(2)}, u32[]{:S(2)}) %collective-permute-start.3) | collective-permute-done | bytes 262176 | tf_op jit(solution)/shard_map/ppermute | solution.py:17
  71.8 12.3 %collective-permute-start.4 = (bf16[256,512]{1,0:T(8,128)(2,1)S(1)}, bf16[256,512]{1,0:T(8,128)(2,1)S(1)}, u32[]{:S(2)}, u32[]{:S(2)}) collective-permute-start(bf16[256,512]{1,0:T(8,128)(2,1)S(1)} %collective-permute-done.3), channel_id=1, source_target_pairs={{0,4},{4,8},{8,12},{1,5},{5,9},{9,13},{2,6},{6,10},{10,14},{3,7},{... | collective-permute-start | bytes 786440 | tf_op jit(solution)/shard_map/ppermute | solution.py:17
  84.1 9.6 %collective-permute-done.4 = bf16[256,512]{1,0:T(8,128)(2,1)S(1)} collective-permute-done((bf16[256,512]{1,0:T(8,128)(2,1)S(1)}, bf16[256,512]{1,0:T(8,128)(2,1)S(1)}, u32[]{:S(2)}, u32[]{:S(2)}) %collective-permute-start.4) | collective-permute-done | bytes 262176 | tf_op jit(solution)/shard_map/ppermute | solution.py:17
  93.7 11.3 %collective-permute-start.5 = (bf16[256,512]{1,0:T(8,128)(2,1)S(1)}, bf16[256,512]{1,0:T(8,128)(2,1)S(1)}, u32[]{:S(2)}, u32[]{:S(2)}) collective-permute-start(bf16[256,512]{1,0:T(8,128)(2,1)S(1)} %collective-permute-done.4), channel_id=1, source_target_pairs={{0,4},{4,8},{8,12},{1,5},{5,9},{9,13},{2,6},{6,10},{10,14},{3,7},{... | collective-permute-start | bytes 786440 | tf_op jit(solution)/shard_map/ppermute | solution.py:17
  105.0 9.7 %collective-permute-done.5 = bf16[256,512]{1,0:T(8,128)(2,1)S(1)} collective-permute-done((bf16[256,512]{1,0:T(8,128)(2,1)S(1)}, bf16[256,512]{1,0:T(8,128)(2,1)S(1)}, u32[]{:S(2)}, u32[]{:S(2)}) %collective-permute-start.5) | collective-permute-done | bytes 262176 | tf_op jit(solution)/shard_map/ppermute | solution.py:17
  114.6 13.8 %collective-permute-start.6 = (bf16[256,512]{1,0:T(8,128)(2,1)S(1)}, bf16[256,512]{1,0:T(8,128)(2,1)S(1)}, u32[]{:S(2)}, u32[]{:S(2)}) collective-permute-start(bf16[256,512]{1,0:T(8,128)(2,1)S(1)} %collective-permute-done.5), channel_id=1, source_target_pairs={{0,4},{4,8},{8,12},{1,5},{5,9},{9,13},{2,6},{6,10},{10,14},{3,7},{... | collective-permute-start | bytes 786440 | tf_op jit(solution)/shard_map/ppermute | solution.py:17
  128.7 9.4 %collective-permute-done.6 = bf16[256,512]{1,0:T(8,128)(2,1)S(1)} collective-permute-done((bf16[256,512]{1,0:T(8,128)(2,1)S(1)}, bf16[256,512]{1,0:T(8,128)(2,1)S(1)}, u32[]{:S(2)}, u32[]{:S(2)}) %collective-permute-start.6) | collective-permute-done | bytes 262176 | tf_op jit(solution)/shard_map/ppermute | solution.py:17
  138.1 9.9 %collective-permute-start.7 = (bf16[256,512]{1,0:T(8,128)(2,1)S(1)}, bf16[256,512]{1,0:T(8,128)(2,1)S(1)}, u32[]{:S(2)}, u32[]{:S(2)}) collective-permute-start(bf16[256,512]{1,0:T(8,128)(2,1)S(1)} %collective-permute-done.6), channel_id=1, source_target_pairs={{0,4},{4,8},{8,12},{1,5},{5,9},{9,13},{2,6},{6,10},{10,14},{3,7},{... | collective-permute-start | bytes 786440 | tf_op jit(solution)/shard_map/ppermute | solution.py:17
  148.1 9.5 %collective-permute-done.7 = bf16[256,512]{1,0:T(8,128)(2,1)S(1)} collective-permute-done((bf16[256,512]{1,0:T(8,128)(2,1)S(1)}, bf16[256,512]{1,0:T(8,128)(2,1)S(1)}, u32[]{:S(2)}, u32[]{:S(2)}) %collective-permute-start.7) | collective-permute-done | bytes 262176 | tf_op jit(solution)/shard_map/ppermute | solution.py:17
  157.6 13.0 %collective-permute-start.8 = (bf16[256,512]{1,0:T(8,128)(2,1)S(1)}, bf16[256,512]{1,0:T(8,128)(2,1)S(1)}, u32[]{:S(2)}, u32[]{:S(2)}) collective-permute-start(bf16[256,512]{1,0:T(8,128)(2,1)S(1)} %collective-permute-done.7), channel_id=1, source_target_pairs={{0,4},{4,8},{8,12},{1,5},{5,9},{9,13},{2,6},{6,10},{10,14},{3,7},{... | collective-permute-start | bytes 786440 | tf_op jit(solution)/shard_map/ppermute | solution.py:17
  172.2 8.0 %collective-permute-done.8 = bf16[256,512]{1,0:T(8,128)(2,1)S(1)} collective-permute-done((bf16[256,512]{1,0:T(8,128)(2,1)S(1)}, bf16[256,512]{1,0:T(8,128)(2,1)S(1)}, u32[]{:S(2)}, u32[]{:S(2)}) %collective-permute-start.8) | collective-permute-done | bytes 262176 | tf_op jit(solution)/shard_map/ppermute | solution.py:17
  186.5 6.0 %fusion.8 = bf16[256,4,256]{2,0,1:T(8,128)(2,1)S(1)} fusion(f32[4,256]{1,0:T(4,128)S(1)} %fusion.53, bf16[2304,512]{1,0:T(8,128)(2,1)} %copy-done.12, pred[256,2304]{0,1:T(8,128)(4,1)S(1)} %fusion.7, bf16[32,4,8,256]{3,2,1,0:T(8,128)(2,1)S(1)} %bitcast.79), kind=kOutput, calls=%fused_computation.17 | convolution fusion | flops 2427981056 | bytes 4001792 | tf_op jit(solution)/shard_map/htk,kd->thd/dot_general | solution.py:48
  192.5 6.9 %all-gather.4.cloned.1.call-done = bf16[1024,4096]{1,0:T(8,128)(2,1)} async-done(((bf16[1024,1024]{1,0:T(8,128)(2,1)}), bf16[1024,4096]{1,0:T(8,128)(2,1)}) %all-gather.4.cloned.1.call-update) | async-done | bytes 8388624 | tf_op jit(solution)/shard_map/all_gather | solution.py:93
  199.5 7.1 %convolution_convert_fusion = bf16[256,4096]{1,0:T(8,128)(2,1)} fusion(bf16[256,1024]{0,1:T(8,128)(2,1)S(1)} %bitcast.71, bf16[1024,4096]{1,0:T(8,128)(2,1)} %all-gather.4.cloned.1.call-done), kind=kOutput, calls=%fused_computation.6 | convolution fusion | flops 2148532224 | bytes 11010048 | tf_op jit(solution)/shard_map/dot_general | solution.py:91
  207.6 33.9 %reduce-scatter.2.cloned.1.call-done = bf16[64,4096]{1,0:T(8,128)(2,1)} async-done(((bf16[256,4096]{1,0:T(8,128)(2,1)}), bf16[64,4096]{1,0:T(8,128)(2,1)}) %reduce-scatter.2.cloned.1.call-update) | async-done | bytes 524304 | tf_op jit(solution)/shard_map/reduce_scatter | solution.py:96
  244.8 147.9 %all-gather.8.cloned.1.call-done = bf16[4096,1024]{1,0:T(8,128)(2,1)} async-done(((bf16[1024,1024]{1,0:T(8,128)(2,1)}), bf16[4096,1024]{1,0:T(8,128)(2,1)}) %all-gather.8.cloned.1.call-update) | async-done | bytes 8388624 | tf_op jit(solution)/shard_map/all_gather | solution.py:104
  392.8 22.8 %all-gather.6.cloned.1.call-done = bf16[256,4096]{1,0:T(8,128)(2,1)} async-done(((bf16[64,4096]{1,0:T(8,128)(2,1)}), bf16[256,4096]{1,0:T(8,128)(2,1)}) %all-gather.6.cloned.1.call-update) | async-done | bytes 2097168 | tf_op jit(solution)/shard_map/all_gather | solution.py:100
  415.5 6.3 %convolution_convert_fusion.1 = bf16[256,1024]{1,0:T(8,128)(2,1)S(1)} fusion(bf16[256,4096]{1,0:T(8,128)(2,1)} %all-gather.6.cloned.1.call-done, bf16[4096,1024]{1,0:T(8,128)(2,1)} %all-gather.8.cloned.1.call-done), kind=kOutput, calls=%fused_computation.18 | convolution fusion | flops 2147745792 | bytes 11010048 | tf_op jit(solution)/shard_map/dot_general | solution.py:102
  528.5 16.5 %while.10 = (s32[]{:T(128)}, f32[1024]{0:T(1024)S(1)}, f32[1024]{0:T(1024)S(1)}, f32[1024]{0:T(1024)S(1)}, s32[]{:T(128)}) while((s32[]{:T(128)}, f32[1024]{0:T(1024)S(1)}, f32[1024]{0:T(1024)S(1)}, f32[1024]{0:T(1024)S(1)}, s32[]{:T(128)}) %tuple.63), condition=%wide.region_6.7_spmd, body=%wide.region_5.6_spmd.sunk | while | flops 2050 | bytes 32869 | solution.py:149
  (235 shorter events, 141.8 us)
Async XLA Ops:
  7.2 420.2 %copy-start = (bf16[4,256,256]{2,1,0:T(8,128)(2,1)S(1)}, bf16[4,256,256]{2,1,0:T(8,128)(2,1)}, u32[]{:S(2)}) copy-start(bf16[4,256,256]{2,1,0:T(8,128)(2,1)} %param.22) | copy-start | bytes 1572868
  7.2 121.3 %copy-start.13 = (s32[1024]{0:T(1024)S(1)}, s32[1024]{0:T(1024)}, u32[]{:S(2)}) copy-start(s32[1024]{0:T(1024)} %param.17) | copy-start | bytes 12292
  7.2 192.3 %all-gather.4.cloned.1.call-start = ((), (), s32[]{:S(2)}) async-start(), calls=%async_computation.1 | async-start | bytes 10485760 | tf_op jit(solution)/shard_map/all_gather | solution.py:93
  7.9 233.6 %reduce-scatter.2.cloned.1.call-start = ((), (), s32[]{:S(2)}) async-start(), calls=%async_computation.2 | async-start | bytes 2621440 | tf_op jit(solution)/shard_map/reduce_scatter | solution.py:96
  15.4 12.9 %collective-permute-start.1 = (bf16[256,512]{1,0:T(8,128)(2,1)S(1)}, bf16[256,512]{1,0:T(8,128)(2,1)S(1)}, u32[]{:S(2)}, u32[]{:S(2)}) collective-permute-start(bf16[256,512]{1,0:T(8,128)(2,1)S(1)} %all_gather.12), channel_id=1, source_target_pairs={{0,4},{4,8},{8,12},{1,5},{5,9},{9,13},{2,6},{6,10},{10,14},{3,7},{... | collective-permute-start | bytes 786440 | tf_op jit(solution)/shard_map/ppermute | solution.py:17
  28.3 19.7 %collective-permute-start.2 = (bf16[256,512]{1,0:T(8,128)(2,1)S(1)}, bf16[256,512]{1,0:T(8,128)(2,1)S(1)}, u32[]{:S(2)}, u32[]{:S(2)}) collective-permute-start(bf16[256,512]{1,0:T(8,128)(2,1)S(1)} %collective-permute-done.1), channel_id=1, source_target_pairs={{0,4},{4,8},{8,12},{1,5},{5,9},{9,13},{2,6},{6,10},{10,14},{3,7},{... | collective-permute-start | bytes 786440 | tf_op jit(solution)/shard_map/ppermute | solution.py:17
  48.0 23.8 %collective-permute-start.3 = (bf16[256,512]{1,0:T(8,128)(2,1)S(1)}, bf16[256,512]{1,0:T(8,128)(2,1)S(1)}, u32[]{:S(2)}, u32[]{:S(2)}) collective-permute-start(bf16[256,512]{1,0:T(8,128)(2,1)S(1)} %collective-permute-done.2), channel_id=1, source_target_pairs={{0,4},{4,8},{8,12},{1,5},{5,9},{9,13},{2,6},{6,10},{10,14},{3,7},{... | collective-permute-start | bytes 786440 | tf_op jit(solution)/shard_map/ppermute | solution.py:17
  71.8 21.9 %collective-permute-start.4 = (bf16[256,512]{1,0:T(8,128)(2,1)S(1)}, bf16[256,512]{1,0:T(8,128)(2,1)S(1)}, u32[]{:S(2)}, u32[]{:S(2)}) collective-permute-start(bf16[256,512]{1,0:T(8,128)(2,1)S(1)} %collective-permute-done.3), channel_id=1, source_target_pairs={{0,4},{4,8},{8,12},{1,5},{5,9},{9,13},{2,6},{6,10},{10,14},{3,7},{... | collective-permute-start | bytes 786440 | tf_op jit(solution)/shard_map/ppermute | solution.py:17
  93.7 21.0 %collective-permute-start.5 = (bf16[256,512]{1,0:T(8,128)(2,1)S(1)}, bf16[256,512]{1,0:T(8,128)(2,1)S(1)}, u32[]{:S(2)}, u32[]{:S(2)}) collective-permute-start(bf16[256,512]{1,0:T(8,128)(2,1)S(1)} %collective-permute-done.4), channel_id=1, source_target_pairs={{0,4},{4,8},{8,12},{1,5},{5,9},{9,13},{2,6},{6,10},{10,14},{3,7},{... | collective-permute-start | bytes 786440 | tf_op jit(solution)/shard_map/ppermute | solution.py:17
  114.6 23.4 %collective-permute-start.6 = (bf16[256,512]{1,0:T(8,128)(2,1)S(1)}, bf16[256,512]{1,0:T(8,128)(2,1)S(1)}, u32[]{:S(2)}, u32[]{:S(2)}) collective-permute-start(bf16[256,512]{1,0:T(8,128)(2,1)S(1)} %collective-permute-done.5), channel_id=1, source_target_pairs={{0,4},{4,8},{8,12},{1,5},{5,9},{9,13},{2,6},{6,10},{10,14},{3,7},{... | collective-permute-start | bytes 786440 | tf_op jit(solution)/shard_map/ppermute | solution.py:17
  138.1 19.5 %collective-permute-start.7 = (bf16[256,512]{1,0:T(8,128)(2,1)S(1)}, bf16[256,512]{1,0:T(8,128)(2,1)S(1)}, u32[]{:S(2)}, u32[]{:S(2)}) collective-permute-start(bf16[256,512]{1,0:T(8,128)(2,1)S(1)} %collective-permute-done.6), channel_id=1, source_target_pairs={{0,4},{4,8},{8,12},{1,5},{5,9},{9,13},{2,6},{6,10},{10,14},{3,7},{... | collective-permute-start | bytes 786440 | tf_op jit(solution)/shard_map/ppermute | solution.py:17
  157.6 22.6 %collective-permute-start.8 = (bf16[256,512]{1,0:T(8,128)(2,1)S(1)}, bf16[256,512]{1,0:T(8,128)(2,1)S(1)}, u32[]{:S(2)}, u32[]{:S(2)}) collective-permute-start(bf16[256,512]{1,0:T(8,128)(2,1)S(1)} %collective-permute-done.7), channel_id=1, source_target_pairs={{0,4},{4,8},{8,12},{1,5},{5,9},{9,13},{2,6},{6,10},{10,14},{3,7},{... | collective-permute-start | bytes 786440 | tf_op jit(solution)/shard_map/ppermute | solution.py:17
  206.5 35.0 %copy-start.4 = (bf16[64,4096]{1,0:T(8,128)(2,1)S(1)}, bf16[64,4096]{1,0:T(8,128)(2,1)}, u32[]{:S(2)}) copy-start(bf16[64,4096]{1,0:T(8,128)(2,1)} %param.18) | copy-start | bytes 1572868
  206.6 37.1 %copy-start.14 = (f32[4096]{0:T(1024)S(1)}, f32[4096]{0:T(1024)}, u32[]{:S(2)}) copy-start(f32[4096]{0:T(1024)} %param.27) | copy-start | bytes 49156
  206.6 38.1 %copy-start.25 = (s32[1024]{0:T(1024)S(1)}, s32[1024]{0:T(1024)}, u32[]{:S(2)}) copy-start(s32[1024]{0:T(1024)} %param.26) | copy-start | bytes 12292
  206.6 38.2 %copy-start.24 = (f32[4,1024]{1,0:T(4,128)S(1)}, f32[4,1024]{1,0:T(4,128)}, u32[]{:S(2)}) copy-start(f32[4,1024]{1,0:T(4,128)} %param.21) | copy-start | bytes 49156
  206.6 186.1 %all-gather.8.cloned.1.call-start = ((), (), s32[]{:S(2)}) async-start(), calls=%async_computation.4 | async-start | bytes 10485760 | tf_op jit(solution)/shard_map/all_gather | solution.py:104
  207.3 208.2 %all-gather.6.cloned.1.call-start = ((), (), s32[]{:S(2)}) async-start(), calls=%async_computation.3 | async-start | bytes 2621440 | tf_op jit(solution)/shard_map/all_gather | solution.py:100
  421.9 4.7 collective-permute-start.9
  504.4 8.9 %copy-start.7 = (f32[15,1024]{1,0:T(8,128)S(1)}, f32[15,1024]{1,0:T(8,128)}, u32[]{:S(2)}) copy-start(f32[15,1024]{1,0:T(8,128)} %slice.312) | copy-start | bytes 184324
  504.4 8.9 %copy-start.8 = (f32[15,1024]{1,0:T(8,128)S(1)}, f32[15,1024]{1,0:T(8,128)}, u32[]{:S(2)}) copy-start(f32[15,1024]{1,0:T(8,128)} %slice.345) | copy-start | bytes 184324
  528.5 5.5 collective-permute-start
  534.0 5.5 collective-permute-start
  539.5 5.5 collective-permute-start
  (21 other events, 81.1 us)
Sparse Core Ops, SparseCore 0:
  9.6 189.8 all-gather.3
  206.7 34.7 reduce-scatter.1
  243.1 149.6 all-gather.7
  394.7 20.7 all-gather.5
where the time goes:
time: 557 us; the launch traced here: 554 us
  waiting for transfers between devices  295 us (53%)
  starting transfers between devices  102 us (18%)
  local copies, waits for them, and re-layouts  77.2 us (14%)
  other arithmetic  32.9 us (6%)
  matrix products  24.8 us (4%)
  between operations  14.7 us (3%)
  blocking collectives  7.43 us (1%)
    all_gather x1, waiting for transfers between devices, local(): lax.all_gather(lru_weight, 'ctx', axis=0, tiled=True)  148 us
    ppermute x12, starting transfers between devices, shifted_2(): lax.ppermute(value, axis, [(source, source + steps) for source in range(i...  102 us
    ppermute x12, waiting for transfers between devices, shifted_2(): lax.ppermute(value, axis, [(source, source + steps) for source in range(i...  82.1 us
    slice x52, local copies, waits for them, and re-layouts, local(): lax.associative_scan(chain_link, (keep_factor, driven), axis=0)  61 us
    reduce_scatter x1, waiting for transfers between devices, local(): lax.psum_scatter(head_part.astype(jnp.bfloat16), 'mp', scatter_dimension=...  33.9 us
    all_gather x1, waiting for transfers between devices, local(): lax.all_gather(rms_scaled(resid_out, norm_gain), 'mp', axis=0, tiled=True)  22.8 us
    add x13, other arithmetic, chain_link(): return (former[0] * latter[0], latter[0] * former[1] + latter[1])  13.8 us
  transfers between devices with their start and end apart: 16, of which 16 were waited for; matrix products, arithmetic and copies ran while one was open for 3% of the time, Pallas kernels for 0%

commit v1 on v0

--- a/solution.py
+++ b/solution.py
@@ -9,6 +9,23 @@
 CONV = 4
 LEVELS = 16
 BW = 256
+
+
+def joined_along(pieces, dim):
+    lengths = list(pieces.shape[1:])
+    lengths[dim] *= pieces.shape[0]
+    return jnp.moveaxis(pieces, 0, dim).reshape(lengths)
+
+
+def gather_around(x, axis, dim):
+    peers = lax.axis_size(axis)
+    right = [(i, (i + 1) % peers) for i in range(peers)]
+    pieces = [x]
+    while len(pieces) < peers:
+        pieces.append(lax.ppermute(pieces[-1], axis, right))
+    index = lax.axis_index(axis)
+    pieces = jnp.stack(pieces)[(index - jnp.arange(peers)) % peers]
+    return joined_along(pieces, dim)
 
 
 def shifted_2(value, axis, steps):
@@ -100,9 +117,7 @@
     normed = lax.all_gather(rms_scaled(resid_out, norm_gain), "mp", axis=0, tiled=True)
     channels = lru_weight.shape[1]
     lru_in = jnp.dot(
-        normed,
-        lax.all_gather(lru_weight, "ctx", axis=0, tiled=True),
-        preferred_element_type=jnp.float32,
+        normed, gather_around(lru_weight, "ctx", 0), preferred_element_type=jnp.float32
     ).astype(jnp.bfloat16)
     rim_rows = shifted_2(lru_in[rows_here - (CONV - 1) :], "ctx", 1)
     extended = jnp.concatenate([rim_rows, lru_in], axis=0)

time: 557 us -> 530 us (0.952)
  waiting for transfers between devices: 295 us -> 247 us
  local copies, waits for them, and re-layouts: 77.2 us -> 93.1 us
  other arithmetic: 32.9 us -> 42.5 us
    all_gather x1 -> x0, waiting for transfers between devices: 148 us -> none  [local(): lax.all_gather(lru_weight, 'ctx', axis=0, tiled=True)]
    ppermute x0 -> x3, waiting for transfers between devices: none -> 92.2 us  [gather_around(): pieces.append(lax.ppermute(pieces[-1], axis, right))]
    ppermute x12, waiting for transfers between devices: 82.1 us -> 154 us  [shifted_2(): lax.ppermute(value, axis, [(source, source + steps) for source in range(i...]
    reduce_scatter x1, waiting for transfers between devices: 33.9 us -> 0.01 us  [local(): lax.psum_scatter(head_part.astype(jnp.bfloat16), 'mp', scatter_dimension=...]
    all_gather x1, waiting for transfers between devices: 22.8 us -> 0.01 us  [local(): lax.all_gather(rms_scaled(resid_out, norm_gain), 'mp', axis=0, tiled=True)]
    gather x0 -> x3, local copies, waits for them, and re-layouts: none -> 13.9 us  [gather_around(): pieces = jnp.stack(pieces)[(index - jnp.arange(peers)) % peers]]
    ppermute x12, starting transfers between devices: 102 us -> 92.1 us  [shifted_2(): lax.ppermute(value, axis, [(source, source + steps) for source in range(i...]
    unnamed x0 -> x1, other arithmetic: none -> 7.75 us
  transfers between devices with their start and end apart: 16 -> 18, of which waited for: 16 -> 14; matrix products, arithmetic and copies ran while one was open for 3% -> 9% of each run, Pallas kernels for 0% -> 0%
where the time goes in v1:
time: 530 us; the launch traced here: 527 us
  waiting for transfers between devices  247 us (47%)
  starting transfers between devices  97.3 us (18%)
  local copies, waits for them, and re-layouts  93.1 us (18%)
  other arithmetic  42.5 us (8%)
  matrix products  25.1 us (5%)
  between operations  14.8 us (3%)
  blocking collectives  7.43 us (1%)
    ppermute x12, waiting for transfers between devices, shifted_2(): lax.ppermute(value, axis, [(source, source + steps) for source in range(i...  154 us
    ppermute x3, waiting for transfers between devices, gather_around(): pieces.append(lax.ppermute(pieces[-1], axis, right))  92.2 us
    ppermute x12, starting transfers between devices, shifted_2(): lax.ppermute(value, axis, [(source, source + steps) for source in range(i...  92.1 us
    slice x52, local copies, waits for them, and re-layouts, local(): lax.associative_scan(chain_link, (keep_factor, driven), axis=0)  61 us
    gather x3, local copies, waits for them, and re-layouts, gather_around(): pieces = jnp.stack(pieces)[(index - jnp.arange(peers)) % peers]  13.9 us
    add x13, other arithmetic, chain_link(): return (former[0] * latter[0], latter[0] * former[1] + latter[1])  13.8 us
  transfers between devices with their start and end apart: 18, of which 14 were waited for; matrix products, arithmetic and copies ran while one was open for 9% of the time, Pallas kernels for 0%

profile of v1, /device:TPU:0, one launch (start us, length us, event | category | flops | bytes accessed | tf_op | source)
XLA Modules:
  0.0 527.0 jit_solution(13281096308157906650)
XLA Ops:
  8.0 7.4 %all_gather.9 = bf16[256,512]{1,0:T(8,128)(2,1)S(1)} all-gather(bf16[64,512]{1,0:T(8,128)(2,1)} %param.16), channel_id=1, replica_groups=mesh['groups'=2,'ctx'=4,'mp'=4] {'mp'}, dimensions={0}, use_global_device_ids=true | all-gather | bytes 327680 | tf_op jit(solution)/shard_map/all_gather | solution.py:89
  18.9 9.3 %collective-permute-done.1 = bf16[256,512]{1,0:T(8,128)(2,1)S(1)} collective-permute-done((bf16[256,512]{1,0:T(8,128)(2,1)S(1)}, bf16[256,512]{1,0:T(8,128)(2,1)S(1)}, u32[]{:S(2)}, u32[]{:S(2)}) %collective-permute-start.1) | collective-permute-done | bytes 262176 | tf_op jit(solution)/shard_map/ppermute | solution.py:34
  28.3 8.5 %collective-permute-start.2 = (bf16[256,512]{1,0:T(8,128)(2,1)S(1)}, bf16[256,512]{1,0:T(8,128)(2,1)S(1)}, u32[]{:S(2)}, u32[]{:S(2)}) collective-permute-start(bf16[256,512]{1,0:T(8,128)(2,1)S(1)} %collective-permute-done.1), channel_id=1, source_target_pairs={{0,4},{4,8},{8,12},{1,5},{5,9},{9,13},{2,6},{6,10},{10,14},{3,7},{... | collective-permute-start | bytes 786440 | tf_op jit(solution)/shard_map/ppermute | solution.py:34
  36.8 11.2 %collective-permute-done.2 = bf16[256,512]{1,0:T(8,128)(2,1)S(1)} collective-permute-done((bf16[256,512]{1,0:T(8,128)(2,1)S(1)}, bf16[256,512]{1,0:T(8,128)(2,1)S(1)}, u32[]{:S(2)}, u32[]{:S(2)}) %collective-permute-start.2) | collective-permute-done | bytes 262176 | tf_op jit(solution)/shard_map/ppermute | solution.py:34
  48.0 13.6 %collective-permute-start.3 = (bf16[256,512]{1,0:T(8,128)(2,1)S(1)}, bf16[256,512]{1,0:T(8,128)(2,1)S(1)}, u32[]{:S(2)}, u32[]{:S(2)}) collective-permute-start(bf16[256,512]{1,0:T(8,128)(2,1)S(1)} %collective-permute-done.2), channel_id=1, source_target_pairs={{0,4},{4,8},{8,12},{1,5},{5,9},{9,13},{2,6},{6,10},{10,14},{3,7},{... | collective-permute-start | bytes 786440 | tf_op jit(solution)/shard_map/ppermute | solution.py:34
  61.6 10.2 %collective-permute-done.3 = bf16[256,512]{1,0:T(8,128)(2,1)S(1)} collective-permute-done((bf16[256,512]{1,0:T(8,128)(2,1)S(1)}, bf16[256,512]{1,0:T(8,128)(2,1)S(1)}, u32[]{:S(2)}, u32[]{:S(2)}) %collective-permute-start.3) | collective-permute-done | bytes 262176 | tf_op jit(solution)/shard_map/ppermute | solution.py:34
  71.8 12.3 %collective-permute-start.4 = (bf16[256,512]{1,0:T(8,128)(2,1)S(1)}, bf16[256,512]{1,0:T(8,128)(2,1)S(1)}, u32[]{:S(2)}, u32[]{:S(2)}) collective-permute-start(bf16[256,512]{1,0:T(8,128)(2,1)S(1)} %collective-permute-done.3), channel_id=1, source_target_pairs={{0,4},{4,8},{8,12},{1,5},{5,9},{9,13},{2,6},{6,10},{10,14},{3,7},{... | collective-permute-start | bytes 786440 | tf_op jit(solution)/shard_map/ppermute | solution.py:34
  84.1 9.6 %collective-permute-done.4 = bf16[256,512]{1,0:T(8,128)(2,1)S(1)} collective-permute-done((bf16[256,512]{1,0:T(8,128)(2,1)S(1)}, bf16[256,512]{1,0:T(8,128)(2,1)S(1)}, u32[]{:S(2)}, u32[]{:S(2)}) %collective-permute-start.4) | collective-permute-done | bytes 262176 | tf_op jit(solution)/shard_map/ppermute | solution.py:34
  93.7 11.4 %collective-permute-start.5 = (bf16[256,512]{1,0:T(8,128)(2,1)S(1)}, bf16[256,512]{1,0:T(8,128)(2,1)S(1)}, u32[]{:S(2)}, u32[]{:S(2)}) collective-permute-start(bf16[256,512]{1,0:T(8,128)(2,1)S(1)} %collective-permute-done.4), channel_id=1, source_target_pairs={{0,4},{4,8},{8,12},{1,5},{5,9},{9,13},{2,6},{6,10},{10,14},{3,7},{... | collective-permute-start | bytes 786440 | tf_op jit(solution)/shard_map/ppermute | solution.py:34
  105.0 9.6 %collective-permute-done.5 = bf16[256,512]{1,0:T(8,128)(2,1)S(1)} collective-permute-done((bf16[256,512]{1,0:T(8,128)(2,1)S(1)}, bf16[256,512]{1,0:T(8,128)(2,1)S(1)}, u32[]{:S(2)}, u32[]{:S(2)}) %collective-permute-start.5) | collective-permute-done | bytes 262176 | tf_op jit(solution)/shard_map/ppermute | solution.py:34
  114.7 13.8 %collective-permute-start.6 = (bf16[256,512]{1,0:T(8,128)(2,1)S(1)}, bf16[256,512]{1,0:T(8,128)(2,1)S(1)}, u32[]{:S(2)}, u32[]{:S(2)}) collective-permute-start(bf16[256,512]{1,0:T(8,128)(2,1)S(1)} %collective-permute-done.5), channel_id=1, source_target_pairs={{0,4},{4,8},{8,12},{1,5},{5,9},{9,13},{2,6},{6,10},{10,14},{3,7},{... | collective-permute-start | bytes 786440 | tf_op jit(solution)/shard_map/ppermute | solution.py:34
  131.3 9.6 %collective-permute-done.6 = bf16[256,512]{1,0:T(8,128)(2,1)S(1)} collective-permute-done((bf16[256,512]{1,0:T(8,128)(2,1)S(1)}, bf16[256,512]{1,0:T(8,128)(2,1)S(1)}, u32[]{:S(2)}, u32[]{:S(2)}) %collective-permute-start.6) | collective-permute-done | bytes 262176 | tf_op jit(solution)/shard_map/ppermute | solution.py:34
  140.8 10.7 %collective-permute-start.7 = (bf16[256,512]{1,0:T(8,128)(2,1)S(1)}, bf16[256,512]{1,0:T(8,128)(2,1)}, u32[]{:S(2)}, u32[]{:S(2)}) collective-permute-start(bf16[256,512]{1,0:T(8,128)(2,1)S(1)} %collective-permute-done.6), channel_id=1, source_target_pairs={{0,4},{4,8},{8,12},{1,5},{5,9},{9,13},{2,6},{6,10},{10,14},{3,7},{... | collective-permute-start | bytes 786440 | tf_op jit(solution)/shard_map/ppermute | solution.py:34
  151.6 86.4 %collective-permute-done.7 = bf16[256,512]{1,0:T(8,128)(2,1)} collective-permute-done((bf16[256,512]{1,0:T(8,128)(2,1)S(1)}, bf16[256,512]{1,0:T(8,128)(2,1)}, u32[]{:S(2)}, u32[]{:S(2)}) %collective-permute-start.7) | collective-permute-done | bytes 262176 | tf_op jit(solution)/shard_map/ppermute | solution.py:34
  250.3 4.7 fusion.56
  254.9 6.3 %fusion.8 = bf16[256,4,256]{2,0,1:T(8,128)(2,1)S(1)} fusion(f32[4,256]{1,0:T(4,128)S(1)} %fusion.56, bf16[2304,512]{1,0:T(8,128)(2,1)} %copy-done.25, pred[256,2304]{0,1:T(8,128)(4,1)} %copy-done.5, bf16[32,4,8,256]{3,2,1,0:T(8,128)(2,1)} %bitcast.88), kind=kOutput, calls=%fused_computation.21 | convolution fusion | flops 2427981056 | bytes 4001792 | tf_op jit(solution)/shard_map/htk,kd->thd/dot_general | solution.py:65
  261.3 7.1 %convolution_convert_fusion = bf16[256,4096]{1,0:T(8,128)(2,1)} fusion(bf16[256,1024]{0,1:T(8,128)(2,1)S(1)} %bitcast.80, bf16[1024,4096]{1,0:T(8,128)(2,1)} %all-gather.3.cloned.1.call-done), kind=kOutput, calls=%fused_computation.10 | convolution fusion | flops 2148532224 | bytes 11010048 | tf_op jit(solution)/shard_map/dot_general | solution.py:108
  271.1 48.1 %collective-permute-done.10 = bf16[1024,1024]{1,0:T(8,128)(2,1)} collective-permute-done((bf16[1024,1024]{1,0:T(8,128)(2,1)}, bf16[1024,1024]{1,0:T(8,128)(2,1)}, u32[]{:S(2)}, u32[]{:S(2)}) %collective-permute-start.10) | collective-permute-done | bytes 2097184 | tf_op jit(solution)/shard_map/ppermute | solution.py:25
  322.5 44.1 %collective-permute-done.11 = bf16[1024,1024]{1,0:T(8,128)(2,1)} collective-permute-done((bf16[1024,1024]{1,0:T(8,128)(2,1)}, bf16[1024,1024]{1,0:T(8,128)(2,1)}, u32[]{:S(2)}, u32[]{:S(2)}) %collective-permute-start.11) | collective-permute-done | bytes 2097184 | tf_op jit(solution)/shard_map/ppermute | solution.py:25
  374.4 5.1 gather_fusion
  379.4 4.9 gather_fusion.1
  384.4 7.8 %pad_maximum_fusion.1 = bf16[4,1024,1024]{2,1,0:T(8,128)(2,1)} fusion(bf16[4,512,1024]{2,1,0:T(8,128)(2,1)} %gather_fusion.1, bf16[4,512,1024]{2,1,0:T(8,128)(2,1)} %gather_fusion), kind=kLoop, calls=%fused_computation.8 | loop fusion | flops 16777216 | bytes 16777216
  392.1 6.3 %convolution_convert_fusion.1 = bf16[256,1024]{1,0:T(8,128)(2,1)S(1)} fusion(bf16[256,4096]{1,0:T(8,128)(2,1)} %all-gather.5.cloned.1.call-done, bf16[4096,1024]{1,0:T(8,128)(2,1)} %bitcast.74), kind=kOutput, calls=%fused_computation.22 | convolution fusion | flops 2147745792 | bytes 11010048 | tf_op jit(solution)/shard_map/dot_general | solution.py:119
  501.2 16.5 %while.10 = (s32[]{:T(128)}, f32[1024]{0:T(1024)S(1)}, f32[1024]{0:T(1024)S(1)}, f32[1024]{0:T(1024)S(1)}, s32[]{:T(128)}) while((s32[]{:T(128)}, f32[1024]{0:T(1024)S(1)}, f32[1024]{0:T(1024)S(1)}, f32[1024]{0:T(1024)S(1)}, s32[]{:T(128)}) %tuple.62), condition=%wide.region_6.7_spmd, body=%wide.region_5.6_spmd.sunk | while | flops 2050 | bytes 32869 | solution.py:164
  (275 shorter events, 154.0 us)
Async XLA Ops:
  7.2 394.7 %copy-start = (bf16[4,256,256]{2,1,0:T(8,128)(2,1)S(1)}, bf16[4,256,256]{2,1,0:T(8,128)(2,1)}, u32[]{:S(2)}) copy-start(bf16[4,256,256]{2,1,0:T(8,128)(2,1)} %param.22) | copy-start | bytes 1572868
  7.2 121.4 %copy-start.3 = (bf16[1024,1024]{1,0:T(8,128)(2,1)S(1)}, bf16[1024,1024]{1,0:T(8,128)(2,1)}, u32[]{:S(2)}) copy-start(bf16[1024,1024]{1,0:T(8,128)(2,1)} %param.20) | copy-start | bytes 6291460
  7.2 123.9 %copy-start.26 = (s32[1024]{0:T(1024)S(1)}, s32[1024]{0:T(1024)}, u32[]{:S(2)}) copy-start(s32[1024]{0:T(1024)} %param.17) | copy-start | bytes 12292
  7.2 254.1 %all-gather.3.cloned.1.call-start = ((), (), s32[]{:S(2)}) async-start(), calls=%async_computation.1 | async-start | bytes 10485760 | tf_op jit(solution)/shard_map/all_gather | solution.py:110
  7.9 311.2 %reduce-scatter.2.cloned.1.call-start = ((), (), s32[]{:S(2)}) async-start(), calls=%async_computation.2 | async-start | bytes 2621440 | tf_op jit(solution)/shard_map/reduce_scatter | solution.py:113
  15.4 12.9 %collective-permute-start.1 = (bf16[256,512]{1,0:T(8,128)(2,1)S(1)}, bf16[256,512]{1,0:T(8,128)(2,1)S(1)}, u32[]{:S(2)}, u32[]{:S(2)}) collective-permute-start(bf16[256,512]{1,0:T(8,128)(2,1)S(1)} %all_gather.9), channel_id=1, source_target_pairs={{0,4},{4,8},{8,12},{1,5},{5,9},{9,13},{2,6},{6,10},{10,14},{3,7},{... | collective-permute-start | bytes 786440 | tf_op jit(solution)/shard_map/ppermute | solution.py:34
  28.3 19.7 %collective-permute-start.2 = (bf16[256,512]{1,0:T(8,128)(2,1)S(1)}, bf16[256,512]{1,0:T(8,128)(2,1)S(1)}, u32[]{:S(2)}, u32[]{:S(2)}) collective-permute-start(bf16[256,512]{1,0:T(8,128)(2,1)S(1)} %collective-permute-done.1), channel_id=1, source_target_pairs={{0,4},{4,8},{8,12},{1,5},{5,9},{9,13},{2,6},{6,10},{10,14},{3,7},{... | collective-permute-start | bytes 786440 | tf_op jit(solution)/shard_map/ppermute | solution.py:34
  48.0 23.8 %collective-permute-start.3 = (bf16[256,512]{1,0:T(8,128)(2,1)S(1)}, bf16[256,512]{1,0:T(8,128)(2,1)S(1)}, u32[]{:S(2)}, u32[]{:S(2)}) collective-permute-start(bf16[256,512]{1,0:T(8,128)(2,1)S(1)} %collective-permute-done.2), channel_id=1, source_target_pairs={{0,4},{4,8},{8,12},{1,5},{5,9},{9,13},{2,6},{6,10},{10,14},{3,7},{... | collective-permute-start | bytes 786440 | tf_op jit(solution)/shard_map/ppermute | solution.py:34
  71.8 21.9 %collective-permute-start.4 = (bf16[256,512]{1,0:T(8,128)(2,1)S(1)}, bf16[256,512]{1,0:T(8,128)(2,1)S(1)}, u32[]{:S(2)}, u32[]{:S(2)}) collective-permute-start(bf16[256,512]{1,0:T(8,128)(2,1)S(1)} %collective-permute-done.3), channel_id=1, source_target_pairs={{0,4},{4,8},{8,12},{1,5},{5,9},{9,13},{2,6},{6,10},{10,14},{3,7},{... | collective-permute-start | bytes 786440 | tf_op jit(solution)/shard_map/ppermute | solution.py:34
  93.7 21.0 %collective-permute-start.5 = (bf16[256,512]{1,0:T(8,128)(2,1)S(1)}, bf16[256,512]{1,0:T(8,128)(2,1)S(1)}, u32[]{:S(2)}, u32[]{:S(2)}) collective-permute-start(bf16[256,512]{1,0:T(8,128)(2,1)S(1)} %collective-permute-done.4), channel_id=1, source_target_pairs={{0,4},{4,8},{8,12},{1,5},{5,9},{9,13},{2,6},{6,10},{10,14},{3,7},{... | collective-permute-start | bytes 786440 | tf_op jit(solution)/shard_map/ppermute | solution.py:34
  114.7 127.8 %copy-start.17 = (bf16[256,512]{1,0:T(8,128)(2,1)}, bf16[256,512]{1,0:T(8,128)(2,1)S(1)}, u32[]{:S(2)}) copy-start(bf16[256,512]{1,0:T(8,128)(2,1)S(1)} %collective-permute-done.5) | copy-start | bytes 786436
  114.7 26.1 %collective-permute-start.6 = (bf16[256,512]{1,0:T(8,128)(2,1)S(1)}, bf16[256,512]{1,0:T(8,128)(2,1)S(1)}, u32[]{:S(2)}, u32[]{:S(2)}) collective-permute-start(bf16[256,512]{1,0:T(8,128)(2,1)S(1)} %collective-permute-done.5), channel_id=1, source_target_pairs={{0,4},{4,8},{8,12},{1,5},{5,9},{9,13},{2,6},{6,10},{10,14},{3,7},{... | collective-permute-start | bytes 786440 | tf_op jit(solution)/shard_map/ppermute | solution.py:34
  128.6 139.9 %collective-permute-start.9 = (bf16[1024,1024]{1,0:T(8,128)(2,1)S(1)}, bf16[1024,1024]{1,0:T(8,128)(2,1)}, u32[]{:S(2)}, u32[]{:S(2)}) collective-permute-start(bf16[1024,1024]{1,0:T(8,128)(2,1)S(1)} %copy-done.3), channel_id=1, source_target_pairs={{0,4},{4,8},{8,12},{12,0},{1,5},{5,9},{9,13},{13,1},{2,6},{6,10},{... | collective-permute-start | bytes 6291464 | tf_op jit(solution)/shard_map/ppermute | solution.py:25
  140.8 101.7 %copy-start.19 = (bf16[256,512]{1,0:T(8,128)(2,1)}, bf16[256,512]{1,0:T(8,128)(2,1)S(1)}, u32[]{:S(2)}) copy-start(bf16[256,512]{1,0:T(8,128)(2,1)S(1)} %collective-permute-done.6) | copy-start | bytes 786436
  140.8 97.2 %collective-permute-start.7 = (bf16[256,512]{1,0:T(8,128)(2,1)S(1)}, bf16[256,512]{1,0:T(8,128)(2,1)}, u32[]{:S(2)}, u32[]{:S(2)}) collective-permute-start(bf16[256,512]{1,0:T(8,128)(2,1)S(1)} %collective-permute-done.6), channel_id=1, source_target_pairs={{0,4},{4,8},{8,12},{1,5},{5,9},{9,13},{2,6},{6,10},{10,14},{3,7},{... | collective-permute-start | bytes 786440 | tf_op jit(solution)/shard_map/ppermute | solution.py:34
  151.5 97.3 %copy-start.10 = (bf16[256,512]{1,0:T(8,128)(2,1)S(1)}, bf16[256,512]{1,0:T(8,128)(2,1)}, u32[]{:S(2)}) copy-start(bf16[256,512]{1,0:T(8,128)(2,1)} %copy-done.9) | copy-start | bytes 786436
  238.0 8.7 %collective-permute-start.8 = (bf16[256,512]{1,0:T(8,128)(2,1)}, bf16[256,512]{1,0:T(8,128)(2,1)S(1)}, u32[]{:S(2)}, u32[]{:S(2)}) collective-permute-start(bf16[256,512]{1,0:T(8,128)(2,1)} %collective-permute-done.7), channel_id=1, source_target_pairs={{0,4},{4,8},{8,12},{1,5},{5,9},{9,13},{2,6},{6,10},{10,14},{3,7},{... | collective-permute-start | bytes 786440 | tf_op jit(solution)/shard_map/ppermute | solution.py:34
  268.4 123.7 %all-gather.5.cloned.1.call-start = ((), (), s32[]{:S(2)}) async-start(), calls=%async_computation.3 | async-start | bytes 2621440 | tf_op jit(solution)/shard_map/all_gather | solution.py:117
  268.5 50.7 %collective-permute-start.10 = (bf16[1024,1024]{1,0:T(8,128)(2,1)}, bf16[1024,1024]{1,0:T(8,128)(2,1)}, u32[]{:S(2)}, u32[]{:S(2)}) collective-permute-start(bf16[1024,1024]{1,0:T(8,128)(2,1)} %collective-permute-done.9), channel_id=1, source_target_pairs={{0,4},{4,8},{8,12},{12,0},{1,5},{5,9},{9,13},{13,1},{2,6},{6,10},{... | collective-permute-start | bytes 6291464 | tf_op jit(solution)/shard_map/ppermute | solution.py:25
  319.2 47.5 %collective-permute-start.11 = (bf16[1024,1024]{1,0:T(8,128)(2,1)}, bf16[1024,1024]{1,0:T(8,128)(2,1)}, u32[]{:S(2)}, u32[]{:S(2)}) collective-permute-start(bf16[1024,1024]{1,0:T(8,128)(2,1)} %collective-permute-done.10), channel_id=1, source_target_pairs={{0,4},{4,8},{8,12},{12,0},{1,5},{5,9},{9,13},{13,1},{2,6},{6,10},{... | collective-permute-start | bytes 6291464 | tf_op jit(solution)/shard_map/ppermute | solution.py:25
  398.5 2.6 collective-permute-start.12
  501.2 5.5 %collective-permute-start = (f32[1024]{0:T(1024)S(1)}, f32[1024]{0:T(1024)S(1)}, u32[]{:S(2)}, u32[]{:S(2)}) collective-permute-start(f32[1024]{0:T(1024)S(1)} %multiply_add_fusion.9), channel_id=1, source_target_pairs={{0,4},{4,8},{8,12},{1,5},{5,9},{9,13},{2,6},{6,10},{10,14},{3,7},{... | collective-permute-start | bytes 12296 | tf_op jit(solution)/shard_map/while/body/eval_jaxpr/ppermute | solution.py:34
  506.7 5.5 %collective-permute-start = (f32[1024]{0:T(1024)S(1)}, f32[1024]{0:T(1024)S(1)}, u32[]{:S(2)}, u32[]{:S(2)}) collective-permute-start(f32[1024]{0:T(1024)S(1)} %multiply_add_fusion.9), channel_id=1, source_target_pairs={{0,4},{4,8},{8,12},{1,5},{5,9},{9,13},{2,6},{6,10},{10,14},{3,7},{... | collective-permute-start | bytes 12296 | tf_op jit(solution)/shard_map/while/body/eval_jaxpr/ppermute | solution.py:34
  512.2 5.5 %collective-permute-start = (f32[1024]{0:T(1024)S(1)}, f32[1024]{0:T(1024)S(1)}, u32[]{:S(2)}, u32[]{:S(2)}) collective-permute-start(f32[1024]{0:T(1024)S(1)} %multiply_add_fusion.9), channel_id=1, source_target_pairs={{0,4},{4,8},{8,12},{1,5},{5,9},{9,13},{2,6},{6,10},{10,14},{3,7},{... | collective-permute-start | bytes 12296 | tf_op jit(solution)/shard_map/while/body/eval_jaxpr/ppermute | solution.py:34
  (38 other events, 891.1 us)
Sparse Core Ops, SparseCore 0:
  9.6 229.0 all-gather.2
  268.5 34.7 reduce-scatter.1
  322.4 24.0 all-gather.4
